TPU v7x, 128 devices: a whole 4x4x4 slice. The times are simulated.
128 devices in a mesh: user: 4 (over x_hi, core), tok: 32 (over z, y, x_lo).
Axes of the slice: x: 4 (x_hi: 2, x_lo: 2; x = x_hi * 2 + x_lo), y: 4, z: 4, core: 2. Of those that a mesh axis runs over, the one named last changes fastest.
Arguments:
- hidden: bfloat16 [4, 4096, 16384], P('user', 'tok'), may hold values from -256 to 256, as said below
- cotangent: bfloat16 [4, 4096, 2048], P('user', 'tok'), may hold values from -6 to 6
- lengths: int32 [4], P('user'), may hold values from 1024 to 4096
Outputs:
- clipped_sum: float32 [16384, 2048], P('tok', 'user')
Inputs may be any that keep to these rules, and one draw needn't show every extreme that they name: bfloat16 activations of mixed magnitudes across tokens and hidden units.
All inputs are finite; a program needn't handle non-finite values.
Results may differ from a plain program's by a relative error of at most 0.0003.
Values may be sent and summed in bfloat16 or wider, within the bound.
A program may use at most 128 MiB of HBM per device.

v0:
```python
import math

import jax
import jax.numpy as jnp
from jax import lax
from jax.sharding import PartitionSpec as P

epsilon = 1e-06


def contract(left, right):
    return lax.dot_general(
        left, right, (((0,), (0,)), ((), ())), preferred_element_type=jnp.float32
    )


def body(hidden, cotangent, lengths):
    tok_count = lax.axis_size("tok")
    user_count = lax.axis_size("user")
    tok_rows = hidden.shape[1]
    hidden_width = hidden.shape[2]
    model_width = cotangent.shape[2]
    capacity = tok_rows * tok_count
    clip_bound = math.sqrt(8.0 * hidden_width * model_width * capacity)
    scaling = math.sqrt(hidden_width * model_width) / (user_count * clip_bound)
    position = lax.axis_index("tok") * tok_rows + lax.iota(jnp.int32, tok_rows)
    keep_rows = position < lengths[0]
    masked = jnp.where(keep_rows[:, None], cotangent[0], jnp.zeros_like(cotangent[0]))
    columns = lax.all_to_all(hidden[0], "tok", split_axis=1, concat_axis=0, tiled=True)
    gathered = lax.all_gather(masked, "tok", axis=0, tiled=True)
    gradient = contract(columns, gathered)
    partial_value = jnp.sum(gradient * gradient)
    norm_sq = lax.psum(partial_value, "tok")
    factor = jnp.minimum(1.0, clip_bound / jnp.sqrt(norm_sq + epsilon)) * scaling
    result = lax.psum_scatter(gradient * factor, "user", scatter_dimension=1, tiled=True)
    return result


def solution(mesh):
    return jax.shard_map(
        body,
        mesh=mesh,
        in_specs=(P("user", "tok", None), P("user", "tok", None), P("user")),
        out_specs=P("tok", "user"),
        check_vma=False,
    )
```

profile of v0, /device:TPU:1, one launch (start us, length us, event | category | flops | bytes accessed | tf_op | source)
XLA Modules:
  0.0 578.5 jit_solution(17392998720566066784)
XLA Ops:
  6.5 0.0 all-gather.2.cloned.1.call-start
  7.2 1.9 bitcast_select_fusion
  9.1 0.0 all-gather.2.cloned.1.call-update
  9.2 0.0 reduce-scatter.2.cloned.1.call-start
  9.2 6.4 %copy.6 = bf16[1,128,16384]{1,2,0:T(8,128)(2,1)} copy(bf16[1,128,16384]{2,1,0:T(8,128)(2,1)} %param.3) | data formatting | bytes 8388608 | tf_op args[0]
  15.6 106.3 %all_to_all.19 = bf16[128,32,512]{0,2,1:T(8,128)(2,1)} all-to-all(bf16[128,32,512]{0,2,1:T(8,128)(2,1)} %bitcast.12), channel_id=1, replica_groups=mesh['user'=4,'tok'=32] {'tok'}, dimensions={1} | all-to-all | bytes 8388608 | tf_op jit(solution)/shard_map/all_to_all | solution.py:29
  122.0 6.5 %copy.7 = bf16[32,128,512]{2,1,0:T(8,128)(2,1)} copy(bf16[32,128,512]{1,2,0:T(8,128)(2,1)} %bitcast.11) | data formatting | bytes 8388608 | tf_op jit(solution)/shard_map/all_to_all | solution.py:29
  128.5 292.3 %all-gather.2.cloned.1.call-done = bf16[4096,2048]{1,0:T(8,128)(2,1)} async-done(((bf16[128,2048]{1,0:T(8,128)(2,1)}), bf16[4096,2048]{1,0:T(8,128)(2,1)}) %all-gather.2.cloned.1.call-update) | async-done | bytes 16777232 | tf_op jit(solution)/shard_map/all_gather | solution.py:30
  420.8 15.8 %multiply_reduce_fusion = (f32[]{:T(128)}, f32[2048,512]{1,0:T(8,128)}) fusion(bf16[4096,2048]{1,0:T(8,128)(2,1)} %all-gather.2.cloned.1.call-done, bf16[4096,512]{1,0:T(8,128)(2,1)} %bitcast.13), kind=kOutput, calls=%fused_computation.1 | convolution fusion | flops 8592031744 | bytes 25165828 | tf_op jit(solution)/shard_map/dot_general | solution.py:12
  436.6 64.9 %psum.7 = f32[]{:T(128)} all-reduce(f32[]{:T(128)} %get-tuple-element.5), channel_id=1, replica_groups=mesh['user'=4,'tok'=32] {'tok'}, use_global_device_ids=true, to_apply=%region_1.2 | all-reduce | flops 1 | bytes 8 | tf_op jit(solution)/shard_map/psum | solution.py:33
  502.2 4.6 multiply_bitcast_fusion
  506.8 0.0 reduce-scatter.2.cloned.1.call-update
  506.9 62.3 %reduce-scatter.2.cloned.1.call-done = f32[512,512]{0,1:T(8,128)} async-done(((f32[512,2048]{0,1:T(8,128)}), f32[512,512]{0,1:T(8,128)}) %reduce-scatter.2.cloned.1.call-update) | async-done | bytes 1048592 | tf_op jit(solution)/shard_map/reduce_scatter | solution.py:35
  569.1 2.5 copy.8
  (1 shorter events, 0.0 us)
Async XLA Ops:
  6.5 414.2 %all-gather.2.cloned.1.call-start = ((), (), s32[]{:S(2)}) async-start(), calls=%async_computation.2 | async-start | bytes 17301504 | tf_op jit(solution)/shard_map/all_gather | solution.py:30
  9.2 560.0 %reduce-scatter.2.cloned.1.call-start = ((), (), s32[]{:S(2)}) async-start(), calls=%async_computation.3 | async-start | bytes 5242880 | tf_op jit(solution)/shard_map/reduce_scatter | solution.py:35
Sparse Core Ops, SparseCore 0:
  9.3 411.4 all-gather.1
  507.0 62.0 reduce-scatter.1
where the time goes:
time: 579 us; the launch traced here: 578 us
  waiting for transfers between devices  355 us (61%)
  blocking collectives  171 us (30%)
  matrix products  15.8 us (3%)
  local copies, waits for them, and re-layouts  15.5 us (3%)
  between operations  14.8 us (3%)
  other arithmetic  6.56 us (1%)
    all_gather x1, waiting for transfers between devices, body(): gathered = lax.all_gather(masked, 'tok', axis=0, tiled=True)  292 us
    all_to_all x1, blocking collectives, body(): lax.all_to_all(hidden[0], 'tok', split_axis=1, concat_axis=0, tiled=True)  106 us
    psum x1, blocking collectives, body(): norm_sq = lax.psum(partial_value, 'tok')  64.9 us
    reduce_scatter x1, waiting for transfers between devices, body(): lax.psum_scatter(gradient * factor, 'user', scatter_dimension=1, tiled=True)  62.3 us
    dot_general x1, matrix products, contract(): lax.dot_general(left, right, (((0,), (0,)), ((), ())), preferred_element_...  15.8 us
  transfers between devices with their start and end apart: 2, of which 2 were waited for; matrix products, arithmetic and copies ran while one was open for 2% of the time, Pallas kernels for 0%

commit v1 on v0

v1 whole, which is shorter than its diff:
```python
import functools
import math

import jax
import jax.numpy as jnp
from jax import lax
from jax.experimental import pallas as pl
from jax.experimental.pallas import tpu as pltpu
from jax.sharding import PartitionSpec as P

epsilon = 1e-06
MESH = pl.DeviceIdType.MESH
LEVELS = 32767.0


def device(xh, xl, y, z, core):
    return (xh * 2 + core, (z * 4 + y) * 2 + xl)


def remote(src, dst, send, recv, where):
    return pltpu.make_async_remote_copy(
        src_ref=src, dst_ref=dst, send_sem=send, recv_sem=recv, device_id=where, device_id_type=MESH
    )


def take(ref, sem):
    pltpu.make_async_copy(ref, ref, sem).wait()


def coded(block):
    peak = jnp.max(jnp.abs(block), axis=0, keepdims=True)
    ok = peak > 1e-30
    step = jnp.where(ok, peak * (1.0 / LEVELS), 0.0)
    inverse = jnp.where(ok, LEVELS / jnp.where(ok, peak, 1.0), 0.0)
    code = jnp.round(block * inverse).astype(jnp.int32).astype(jnp.int16)
    return code, step


def kernel(
    clip_bound, scaling,
    lengths, hidden, cotangent, out,
    masked, cols, rows, turned, t_code, t_step, t_got, t_gotstep,
    x_code, x_step, x_got, x_gotstep, square, near, far,
    swap_s, swap_r, ring_s, ring_r, side_s, side_r, rows_s, rows_r,
    ts_s, ts_r, tt_s, tt_r, xs_s, xs_r, xt_s, xt_r, near_s, near_r, far_s, far_r,
):
    user, tok = lax.axis_index("user"), lax.axis_index("tok")
    xh, core = user // 2, user % 2
    xl, y, z = tok % 2, (tok // 2) % 4, tok // 8
    zi = z % 2
    zmate = z + 1 - 2 * zi
    ztwin = 3 - z
    home = xl == core
    up, down, across = (y + 1) % 4, (y + 3) % 4, (y + 2) % 4
    shard = zi * 4 + y

    def send_rows(kind, k):
        slot = kind * 2 + k
        for dy, dz, cc in [(1, 0, 0), (3, 1, 1), (2, 0, 1), (0, 1, 0), (3, 0, 0), (1, 1, 1), (0, 1, 1), (2, 1, 0),
                           (1, 0, 1), (3, 1, 0), (2, 0, 0), (3, 0, 1), (2, 1, 1), (1, 1, 0), (0, 0, 0), (0, 0, 1)]:
            y2 = (y + dy) % 4
            z2 = zmate if dz else z
            zrow = z2 if kind else 3 - z2
            start = ((zrow * 4 + y2) * 2 + cc) * 512 + k * 256
            src = hidden.at[0, :, pl.ds(pl.multiple_of(start, 256), 256)]
            dst = rows.at[slot, shard * 2 + xl]
            where = device(xh, core, y2, z2, cc)
            if dy == 0 and dz == 0:
                mine = jnp.logical_and(home, core == cc)

                @pl.when(mine)
                def _():
                    pltpu.make_async_copy(src, dst, rows_r.at[slot]).start()

                @pl.when(jnp.logical_not(mine))
                def _():
                    remote(src, dst, rows_s.at[slot], rows_r.at[slot], where).start()
            else:
                remote(src, dst, rows_s.at[slot], rows_r.at[slot], where).start()

    token = tok * 128 + lax.broadcasted_iota(jnp.int32, (128, 256), 0)
    keep = token < lengths[0]
    for p in range(8):
        masked[p] = jnp.where(keep, cotangent[0, :, p * 256:(p + 1) * 256], jnp.zeros((128, 256), jnp.bfloat16))

    spot = pl.ds(pl.multiple_of(xl * 128, 128), 128)

    def swap(lane):
        src = masked.at[lane * 4:lane * 4 + 4]
        dst = cols.at[lane * 4:lane * 4 + 4, shard, spot]
        return src, dst

    for lane in (0, 1):
        src, dst = swap(lane)
        mine = jnp.logical_and(home, core == lane)

        @pl.when(mine)
        def _():
            pltpu.make_async_copy(src, dst, swap_r.at[xl]).start()

        @pl.when(jnp.logical_not(mine))
        def _():
            remote(src, dst, swap_s.at[lane], swap_r.at[xl], device(xh, core, y, z, lane)).start()

    send_rows(0, 0)

    for half in (0, 1):
        take(masked.at[0:4], swap_r.at[half])

    def piece(p, which, part=None):
        ref = cols.at[p, which]
        if part is None:
            return ref
        return ref.at[part * 128:part * 128 + 128]

    def pass_on(p, which, sem, where, part=None):
        ref = piece(p, which, part)
        remote(ref, ref, ring_s, ring_r.at[sem], where).start()

    def got(p, sem, part=None):
        take(piece(p, 0, part), ring_r.at[sem])

    @pl.when(core == 0)
    def _():
        here = lambda y2, z2: device(xh, xl, y2, z2, 0)
        for p in range(4):
            pass_on(p, shard, p, here(y, zmate))
            pass_on(p, shard, 4 + p, here(up, z))
            pass_on(p, shard, 12 + p, here(down, z))
        send_rows(0, 1)
        mate = (1 - zi) * 4
        for p in range(4):
            got(p, p)
            pass_on(p, mate + y, 8 + p, here(up, z))
            pass_on(p, mate + y, 16 + p, here(down, z))
        for m in (0, 1):
            base = mate if m else zi * 4
            for p in range(4):
                got(p, 4 + m * 4 + p)
                pass_on(p, base + down, 20 + m * 4 + p, here(up, z), 0)
                got(p, 12 + m * 4 + p)
                pass_on(p, base + up, 28 + m * 4 + p, here(down, z), 1)
        for p in range(4):
            for m in (0, 1):
                got(p, 20 + m * 4 + p, 0)
                got(p, 28 + m * 4 + p, 1)
            remote(cols.at[p], cols.at[p], side_s.at[p], side_r.at[p], device(xh, xl, y, z, 1)).start()

    @pl.when(core == 1)
    def _():
        here = lambda y2, z2: device(xh, xl, y2, z2, 1)
        own = zi * 4
        for p in range(4):
            pass_on(4 + p, shard, p, here(up, z))
            pass_on(4 + p, shard, 4 + p, here(down, z))
            pass_on(4 + p, shard, 16 + p, here(y, zmate))
        send_rows(0, 1)
        for p in range(4):
            got(4 + p, p)
            pass_on(4 + p, own + down, 8 + p, here(up, z), 0)
            pass_on(4 + p, own + down, 20 + p, here(y, zmate))
            got(4 + p, 4 + p)
            pass_on(4 + p, own + up, 12 + p, here(down, z), 1)
            pass_on(4 + p, own + up, 24 + p, here(y, zmate))
        for p in range(4):
            got(4 + p, 8 + p, 0)
            got(4 + p, 12 + p, 1)
            pass_on(4 + p, own + across, 28 + p, here(y, zmate))
        for p in range(4):
            for kind in range(4):
                got(4 + p, 16 + kind * 4 + p)
            remote(cols.at[4 + p], cols.at[4 + p], side_s.at[p], side_r.at[p], device(xh, xl, y, z, 0)).start()

    send_rows(1, 0)
    for p in range(4):
        take(cols.at[0], side_r.at[p])
    send_rows(1, 1)

    def turn(slot):
        take(rows.at[slot], rows_r.at[slot])
        for s in range(16):
            turned[:, s * 128:(s + 1) * 128] = rows[slot, s].T

    def product(piece_at):
        right = cols[piece_at].reshape(2048, 256)
        return lax.dot_general(turned[...], right, (((1,), (0,)), ((), ())), preferred_element_type=jnp.float32)

    def target(jj):
        return jnp.where(jj < 2, 1 - xh, xh), jj % 2

    twin = device(xh, xl, y, ztwin, core)

    def t_data(k, jj):
        return remote(t_code.at[k, jj], t_got.at[k, jj], ts_s.at[k, jj], ts_r.at[k, jj], twin)

    def t_scale(k, jj):
        return remote(t_step.at[k, jj], t_gotstep.at[k, jj], tt_s.at[k, jj], tt_r.at[k, jj], twin)

    def t_pass(k, carry):
        turn(k)

        def one(jj, inner):
            xt, jc = target(jj)
            for h in (0, 1):
                code, step = coded(product((xt * 2 + jc) * 2 + h))
                t_code[k, jj, h] = code
                t_step[k, jj, h] = jnp.broadcast_to(step, (8, 256))
            t_data(k, jj).start()
            t_scale(k, jj).start()
            return inner

        return lax.fori_loop(0, 4, one, carry)

    lax.fori_loop(0, 2, t_pass, 0)

    square[...] = jnp.zeros_like(square)
    slot_x = xh * 2 + xl

    def x_parts(k, jj):
        xt, jc = target(jj)
        mine = jnp.logical_and(jnp.logical_and(xt == xh, home), jc == core)
        where = device(xt, core, y, z, jc)
        data = (x_code.at[k, jj], x_got.at[slot_x, k])
        scale = (x_step.at[k, jj], x_gotstep.at[slot_x, k])
        return mine, where, data, scale

    def o_pass(k, carry):
        turn(2 + k)

        def one(jj, inner):
            xt, jc = target(jj)
            take(t_got.at[k, jj], ts_r.at[k, jj])
            take(t_gotstep.at[k, jj], tt_r.at[k, jj])
            for h in (0, 1):
                value = product((xt * 2 + jc) * 2 + h)
                value = value + t_got[k, jj, h].astype(jnp.int32).astype(jnp.float32) * t_gotstep[k, jj, h, 0:1]
                square[...] += jnp.sum((value * value).reshape(32, 8, 256), axis=0)
                code, step = coded(value)
                x_code[k, jj, h] = code
                x_step[k, jj, h] = jnp.broadcast_to(step, (8, 256))
            mine, where, data, scale = x_parts(k, jj)

            @pl.when(mine)
            def _():
                pltpu.make_async_copy(*data, xs_r.at[slot_x, k]).start()
                pltpu.make_async_copy(*scale, xt_r.at[slot_x, k]).start()

            @pl.when(jnp.logical_not(mine))
            def _():
                remote(*data, xs_s.at[k, jj], xs_r.at[slot_x, k], where).start()
                remote(*scale, xt_s.at[k, jj], xt_r.at[slot_x, k], where).start()

            return inner

        return lax.fori_loop(0, 4, one, carry)

    lax.fori_loop(0, 2, o_pass, 0)

    spot1 = z * 2 + core
    near[spot1] = square[:, 0:128] + square[:, 128:256]
    for dz in range(4):
        for dc in range(2):
            if (dz, dc) != (0, 0):
                remote(near.at[spot1], near.at[spot1], near_s, near_r,
                       device(xh, xl, y, (z + dz) % 4, (core + dc) % 2)).start()
    take(near.at[0:7], near_r)
    spot2 = slot_x * 4 + y
    far[spot2] = jnp.sum(near[...], axis=0)
    for dh in range(2):
        for dl in range(2):
            for dy in range(4):
                if (dh, dl, dy) != (0, 0, 0):
                    remote(far.at[spot2], far.at[spot2], far_s, far_r,
                           device((xh + dh) % 2, (xl + dl) % 2, (y + dy) % 4, z, core)).start()
    take(far.at[0:15], far_r)

    factors = []
    for x in range(4):
        total = jnp.sum(far[x * 4] + far[x * 4 + 1] + far[x * 4 + 2] + far[x * 4 + 3], axis=(0, 1), keepdims=True)
        factors.append(jnp.minimum(1.0, clip_bound / jnp.sqrt(total + epsilon)) * scaling)

    for k in range(2):
        for x in range(4):
            take(x_got.at[x, k], xs_r.at[x, k])
            take(x_gotstep.at[x, k], xt_r.at[x, k])
        for h in (0, 1):
            total = None
            for x in range(4):
                weight = factors[x] * x_gotstep[x, k, h, 0:1]
                term = x_got[x, k, h].astype(jnp.int32).astype(jnp.float32) * weight
                total = term if total is None else total + term
            out[k * 256:(k + 1) * 256, h * 256:(h + 1) * 256] = total

    for lane in (0, 1):
        src, dst = swap(lane)

        @pl.when(jnp.logical_not(jnp.logical_and(home, core == lane)))
        def _():
            take(src, swap_s.at[lane])

    take(cols.at[0:7, 0:4], ring_s)
    for p in range(4):
        take(cols.at[0], side_s.at[p])
    for slot in range(4):
        @pl.when(home)
        def _():
            take(rows.at[slot, 0:15], rows_s.at[slot])

        @pl.when(jnp.logical_not(home))
        def _():
            take(rows.at[slot], rows_s.at[slot])
    for k in range(2):
        for jj in range(4):
            take(t_code.at[k, jj], ts_s.at[k, jj])
            take(t_step.at[k, jj], tt_s.at[k, jj])
            mine = x_parts(k, jj)[0]

            @pl.when(jnp.logical_not(mine))
            def _():
                take(x_code.at[k, jj], xs_s.at[k, jj])
                take(x_step.at[k, jj], xt_s.at[k, jj])
    take(near.at[0:7], near_s)
    take(far.at[0:15], far_s)


def body(hidden, cotangent, lengths):
    tok_count = lax.axis_size("tok")
    user_count = lax.axis_size("user")
    hidden_width = hidden.shape[2]
    model_width = cotangent.shape[2]
    capacity = hidden.shape[1] * tok_count
    clip_bound = math.sqrt(8.0 * hidden_width * model_width * capacity)
    scaling = math.sqrt(hidden_width * model_width) / (user_count * clip_bound)
    half, full, word = jnp.bfloat16, jnp.float32, jnp.int16
    dma = pltpu.SemaphoreType.DMA
    return pl.pallas_call(
        functools.partial(kernel, clip_bound, scaling),
        out_shape=jax.ShapeDtypeStruct((512, 512), full),
        in_specs=[
            pl.BlockSpec(memory_space=pltpu.SMEM),
            pl.BlockSpec(memory_space=pl.ANY),
            pl.BlockSpec(memory_space=pltpu.VMEM),
        ],
        out_specs=pl.BlockSpec(memory_space=pltpu.VMEM),
        scratch_shapes=[
            pltpu.VMEM((8, 128, 256), half),
            pltpu.VMEM((8, 8, 256, 256), half),
            pltpu.VMEM((4, 16, 128, 256), half),
            pltpu.VMEM((256, 2048), half),
            pltpu.VMEM((2, 4, 2, 256, 256), word),
            pltpu.VMEM((2, 4, 2, 8, 256), full),
            pltpu.VMEM((2, 4, 2, 256, 256), word),
            pltpu.VMEM((2, 4, 2, 8, 256), full),
            pltpu.VMEM((2, 4, 2, 256, 256), word),
            pltpu.VMEM((2, 4, 2, 8, 256), full),
            pltpu.VMEM((4, 2, 2, 256, 256), word),
            pltpu.VMEM((4, 2, 2, 8, 256), full),
            pltpu.VMEM((8, 256), full),
            pltpu.VMEM((8, 8, 128), full),
            pltpu.VMEM((16, 8, 128), full),
            dma((2,)), dma((2,)), dma, dma((36,)), dma((4,)), dma((4,)), dma((4,)), dma((4,)),
            dma((2, 4)), dma((2, 4)), dma((2, 4)), dma((2, 4)),
            dma((2, 4)), dma((4, 2)), dma((2, 4)), dma((4, 2)),
            dma, dma, dma, dma,
        ],
        compiler_params=pltpu.CompilerParams(has_side_effects=True, vmem_limit_bytes=56 << 20),
        name="clipped_sum",
    )(lengths, hidden, cotangent)


def solution(mesh):
    return jax.shard_map(
        body,
        mesh=mesh,
        in_specs=(P("user", "tok", None), P("user", "tok", None), P("user")),
        out_specs=P("tok", "user"),
        check_vma=False,
    )
```

time: 579 us -> 143 us (0.25)
  waiting for transfers between devices: 355 us -> 0 us
  blocking collectives: 171 us -> 0 us
  Pallas kernels: 0 us -> 140 us
  matrix products: 15.8 us -> 0 us
  between operations: 14.8 us -> 0.66 us
  local copies, waits for them, and re-layouts: 15.5 us -> 2.26 us
  other arithmetic: 6.56 us -> 0 us
    all_gather x1 -> x0, waiting for transfers between devices: 292 us -> none  [body(): gathered = lax.all_gather(masked, 'tok', axis=0, tiled=True)]
    pallas_call x0 -> x1, Pallas kernels: none -> 140 us  [body(): pl.pallas_call(functools.partial(kernel, clip_bound, scaling), out_shape=...]
    all_to_all x1 -> x0, blocking collectives: 106 us -> none  [body(): lax.all_to_all(hidden[0], 'tok', split_axis=1, concat_axis=0, tiled=True)]
    psum x1 -> x0, blocking collectives: 64.9 us -> none  [body(): norm_sq = lax.psum(partial_value, 'tok')]
    reduce_scatter x1 -> x0, waiting for transfers between devices: 62.3 us -> none  [body(): lax.psum_scatter(gradient * factor, 'user', scatter_dimension=1, tiled=True)]
    dot_general x1 -> x0, matrix products: 15.8 us -> none  [contract(): lax.dot_general(left, right, (((0,), (0,)), ((), ())), preferred_element_...]
    all_to_all x1 -> x0, local copies, waits for them, and re-layouts: 6.53 us -> none  [body(): lax.all_to_all(hidden[0], 'tok', split_axis=1, concat_axis=0, tiled=True)]
  transfers between devices with their start and end apart: 2 -> 0, of which waited for: 2 -> 0; matrix products, arithmetic and copies ran while one was open for 2% -> 0% of each run, Pallas kernels for 0% -> 0%
where the time goes in v1:
time: 143 us
  Pallas kernels  140 us (98%)
  local copies, waits for them, and re-layouts  2.26 us (2%)
    pallas_call x1, Pallas kernels, body(): pl.pallas_call(functools.partial(kernel, clip_bound, scaling), out_shape=...  140 us

profile of v1, /device:TPU:1, one launch (start us, length us, event | category | flops | bytes accessed | tf_op | source)
XLA Modules:
  0.0 142.7 jit_solution(17462859567878697001)
XLA Ops:
  0.7 139.8 %clipped_sum.1 = f32[512,512]{1,0:T(8,128)} custom-call(s32[1]{0:T(128)S(6)} %copy.5.lengths, bf16[1,128,16384]{2,1,0:T(8,128)(2,1)} %hidden.1, bf16[1,128,2048]{2,1,0:T(8,128)(2,1)} %cotangent.1), custom_call_target="tpu_custom_call" | custom-call | tf_op jit(solution)/shard_map/clipped_sum/pallas_call | solution.py:336
  140.5 2.3 %copy.6 = f32[512,512]{1,0:T(8,128)} copy(f32[512,512]{1,0:T(8,128)} %clipped_sum.1) | data formatting | bytes 2097152

commit v2 on v1

v2 whole, which is shorter than its diff:
```python
import functools
import math

import jax
import jax.numpy as jnp
from jax import lax
from jax.experimental import pallas as pl
from jax.experimental.pallas import tpu as pltpu
from jax.sharding import PartitionSpec as P

epsilon = 1e-06
MESH = pl.DeviceIdType.MESH
LEVELS = 32767.0
ORDER = [(1, 0, 0), (3, 1, 1), (2, 0, 1), (0, 1, 0), (3, 0, 0), (1, 1, 1), (0, 1, 1), (2, 1, 0),
         (1, 0, 1), (3, 1, 0), (2, 0, 0), (3, 0, 1), (2, 1, 1), (1, 1, 0), (0, 0, 0), (0, 0, 1)]
PACE = (16, 0, 0, 0, 0, 0, 0, 16, 16, 16, 0, 0, 0)


def device(xh, xl, y, z, core):
    return (xh * 2 + core, (z * 4 + y) * 2 + xl)


def remote(src, dst, send, recv, where):
    return pltpu.make_async_remote_copy(
        src_ref=src, dst_ref=dst, send_sem=send, recv_sem=recv, device_id=where, device_id_type=MESH
    )


def take(ref, sem):
    pltpu.make_async_copy(ref, ref, sem).wait()


def coded(block):
    peak = jnp.max(jnp.abs(block), axis=0, keepdims=True)
    ok = peak > 1e-30
    step = jnp.where(ok, peak * (1.0 / LEVELS), 0.0)
    inverse = jnp.where(ok, LEVELS / jnp.where(ok, peak, 1.0), 0.0)
    code = jnp.round(block * inverse).astype(jnp.int32).astype(jnp.int16)
    return code, step


def kernel(
    clip_bound, scaling,
    lengths, hidden, cotangent, out,
    masked, cols, rows, turned, t_code, t_step, t_got, t_gotstep,
    x_code, x_step, x_got, x_gotstep, square, near, far,
    swap_s, swap_r, ring_s, ring_r, side_s, side_r, rows_s, rows_r,
    ts_s, ts_r, tt_s, tt_r, xs_s, xs_r, xt_s, xt_r, near_s, near_r, far_s, far_r,
):
    user, tok = lax.axis_index("user"), lax.axis_index("tok")
    xh, core = user // 2, user % 2
    xl, y, z = tok % 2, (tok // 2) % 4, tok // 8
    zi = z % 2
    zmate = z + 1 - 2 * zi
    ztwin = 3 - z
    home = xl == core
    up, down, across = (y + 1) % 4, (y + 3) % 4, (y + 2) % 4
    shard = zi * 4 + y

    def send_row(n):
        slot, (dy, dz, cc) = n // 16, ORDER[n % 16]
        kind, k = slot // 2, slot % 2
        y2 = (y + dy) % 4
        z2 = zmate if dz else z
        zrow = z2 if kind else 3 - z2
        start = ((zrow * 4 + y2) * 2 + cc) * 512 + k * 256
        src = hidden.at[0, :, pl.ds(pl.multiple_of(start, 256), 256)]
        dst = rows.at[slot, shard * 2 + xl]
        where = device(xh, core, y2, z2, cc)
        away = remote(src, dst, rows_s.at[slot], rows_r.at[slot], where)
        if dy == 0 and dz == 0:
            mine = jnp.logical_and(home, core == cc)

            @pl.when(mine)
            def _():
                pltpu.make_async_copy(src, dst, rows_r.at[slot]).start()

            pl.when(jnp.logical_not(mine))(away.start)
        else:
            away.start()

    def send_rows(point):
        for n in range(sum(PACE[:point]), sum(PACE[:point + 1])):
            send_row(n)

    barrier = pltpu.get_barrier_semaphore()
    partners = [(xh, (xl + dl) % 2, (y + dy) % 4, z2, (core + dc) % 2)
                for dl in range(2) for dy in range(4) for z2 in (z, zmate) for dc in range(2)][1:]
    partners += [(1 - xh, dl, y, z, dc) for dl in range(2) for dc in range(2)]
    partners += [(h2, dl, y, ztwin, core) for h2 in (xh, 1 - xh) for dl in range(2)]
    for partner in partners:
        pl.semaphore_signal(barrier, inc=1, device_id=device(*partner), device_id_type=MESH)

    token = tok * 128 + lax.broadcasted_iota(jnp.int32, (128, 256), 0)
    keep = token < lengths[0]
    for q in range(8):
        lane, p = q // 4, q % 4
        start = (((1 - xh if p < 2 else xh) * 2 + lane) * 2 + p % 2) * 256
        part = cotangent[0, :, pl.ds(pl.multiple_of(start, 256), 256)]
        masked[q] = jnp.where(keep, part, jnp.zeros((128, 256), jnp.bfloat16))

    pl.semaphore_wait(barrier, len(partners))

    spot = pl.ds(pl.multiple_of(xl * 128, 128), 128)

    def swap(lane):
        src = masked.at[lane * 4:lane * 4 + 4]
        dst = cols.at[lane * 4:lane * 4 + 4, shard, spot]
        return src, dst

    for lane in (0, 1):
        src, dst = swap(lane)
        mine = jnp.logical_and(home, core == lane)

        @pl.when(mine)
        def _():
            pltpu.make_async_copy(src, dst, swap_r.at[xl]).start()

        @pl.when(jnp.logical_not(mine))
        def _():
            remote(src, dst, swap_s.at[lane], swap_r.at[xl], device(xh, core, y, z, lane)).start()

    send_rows(0)

    for half in (0, 1):
        take(masked.at[0:4], swap_r.at[half])

    def piece(p, which, part=None):
        ref = cols.at[p, which]
        if part is None:
            return ref
        return ref.at[part * 128:part * 128 + 128]

    def pass_on(p, which, sem, where, part=None):
        ref = piece(p, which, part)
        remote(ref, ref, ring_s, ring_r.at[sem], where).start()

    def got(p, sem, part=None):
        take(piece(p, 0, part), ring_r.at[sem])

    mate, own = (1 - zi) * 4, zi * 4

    def lane0(step, p):
        here = lambda y2, z2: device(xh, xl, y2, z2, 0)
        if step == 0:
            pass_on(p, shard, p, here(y, zmate))
            pass_on(p, shard, 4 + p, here(up, z))
            pass_on(p, shard, 12 + p, here(down, z))
        if step == 1:
            got(p, p)
            pass_on(p, mate + y, 8 + p, here(up, z))
            pass_on(p, mate + y, 16 + p, here(down, z))
        if step in (1, 2):
            base, m = (own, 0) if step == 1 else (mate, 1)
            got(p, 4 + m * 4 + p)
            pass_on(p, base + down, 20 + m * 4 + p, here(up, z), 0)
            got(p, 12 + m * 4 + p)
            pass_on(p, base + up, 28 + m * 4 + p, here(down, z), 1)
        if step == 3:
            for m in (0, 1):
                got(p, 20 + m * 4 + p, 0)
                got(p, 28 + m * 4 + p, 1)
            remote(cols.at[p], cols.at[p], side_s.at[p], side_r.at[p], device(xh, xl, y, z, 1)).start()

    def lane1(step, p):
        here = lambda y2, z2: device(xh, xl, y2, z2, 1)
        if step == 0:
            pass_on(4 + p, shard, p, here(up, z))
            pass_on(4 + p, shard, 4 + p, here(down, z))
            pass_on(4 + p, shard, 16 + p, here(y, zmate))
        if step == 1:
            got(4 + p, p)
            pass_on(4 + p, own + down, 8 + p, here(up, z), 0)
            pass_on(4 + p, own + down, 20 + p, here(y, zmate))
            got(4 + p, 4 + p)
            pass_on(4 + p, own + up, 12 + p, here(down, z), 1)
            pass_on(4 + p, own + up, 24 + p, here(y, zmate))
        if step == 2:
            got(4 + p, 8 + p, 0)
            got(4 + p, 12 + p, 1)
            pass_on(4 + p, own + across, 28 + p, here(y, zmate))
        if step == 3:
            for kind in range(4):
                got(4 + p, 16 + kind * 4 + p)
            remote(cols.at[4 + p], cols.at[4 + p], side_s.at[p], side_r.at[p], device(xh, xl, y, z, 0)).start()

    def turn(slot):
        take(rows.at[slot], rows_r.at[slot])
        for s in range(16):
            turned[slot, :, s * 128:(s + 1) * 128] = rows[slot, s].T

    def product(left, q):
        right = cols[q].reshape(2048, 256)
        return lax.dot_general(left, right, (((1,), (0,)), ((), ())), preferred_element_type=jnp.float32)

    twin = device(xh, xl, y, ztwin, core)

    def t_data(q, k):
        return remote(t_code.at[q, k], t_got.at[q, k], ts_s.at[q, k], ts_r.at[q, k], twin)

    def t_scale(q, k):
        return remote(t_step.at[q, k], t_gotstep.at[q, k], tt_s.at[q, k], tt_r.at[q, k], twin)

    def t_part(p, k):
        def one(lane, carry):
            q = lane * 4 + p
            code, step = coded(product(turned[k], q))
            t_code[q, k] = code
            t_step[q, k] = jnp.broadcast_to(step, (8, 256))
            t_data(q, k).start()
            t_scale(q, k).start()
            return carry

        lax.fori_loop(0, 2, one, 0)

    for tick in range(8):
        for lane, steps in enumerate((lane0, lane1)):
            @pl.when(core == lane)
            def _():
                for p in range(4):
                    if 0 <= tick - p <= 3:
                        steps(tick - p, p)
        send_rows(1 + tick)
        if tick == 4:
            turn(0)
        if tick >= 4:
            take(cols.at[0], side_r.at[tick - 4])
            t_part(tick - 4, 0)

    turn(1)
    for p in range(4):
        send_rows(9 + p)
        t_part(p, 1)

    square[...] = jnp.zeros_like(square)
    slot_x = xh * 2 + xl

    def x_parts(k, jj):
        xt, jc = (1 - xh if jj < 2 else xh), jj % 2
        mine = jnp.logical_and(home, jc == core) if jj >= 2 else None
        where = device(xt, core, y, z, jc)
        data = (x_code.at[k, jj], x_got.at[slot_x, k])
        scale = (x_step.at[k, jj], x_gotstep.at[slot_x, k])
        return mine, where, data, scale

    def o_pass(k, carry):
        turn(2 + k)
        for jj in range(4):
            def one(h, inner, jj=jj):
                q = (jj % 2) * 4 + (jj // 2) * 2 + h
                value = product(turned[2 + k], q)
                take(t_got.at[q, k], ts_r.at[q, k])
                take(t_gotstep.at[q, k], tt_r.at[q, k])
                value = value + t_got[q, k].astype(jnp.int32).astype(jnp.float32) * t_gotstep[q, k, 0:1]
                square[...] += jnp.sum((value * value).reshape(32, 8, 256), axis=0)
                code, step = coded(value)
                x_code[k, jj, h] = code
                x_step[k, jj, h] = jnp.broadcast_to(step, (8, 256))
                return inner

            lax.fori_loop(0, 2, one, 0)
            mine, where, data, scale = x_parts(k, jj)

            def away():
                remote(*data, xs_s.at[k, jj], xs_r.at[slot_x, k], where).start()
                remote(*scale, xt_s.at[k, jj], xt_r.at[slot_x, k], where).start()

            def near_by():
                pltpu.make_async_copy(*data, xs_r.at[slot_x, k]).start()
                pltpu.make_async_copy(*scale, xt_r.at[slot_x, k]).start()

            if mine is None:
                away()
            else:
                pl.when(mine)(near_by)
                pl.when(jnp.logical_not(mine))(away)
        return carry

    lax.fori_loop(0, 2, o_pass, 0)

    spot1 = shard * 2 + core
    near[spot1] = square[:, 0:128] + square[:, 128:256]
    for dy, dz, dc in [(2, 1, 1), (2, 1, 0), (2, 0, 1), (2, 0, 0), (1, 1, 1), (3, 1, 1), (1, 1, 0), (3, 1, 0),
                       (1, 0, 1), (3, 0, 1), (1, 0, 0), (3, 0, 0), (0, 1, 1), (0, 1, 0), (0, 0, 1)]:
        remote(near.at[spot1], near.at[spot1], near_s, near_r,
               device(xh, xl, (y + dy) % 4, zmate if dz else z, (core + dc) % 2)).start()
    take(near.at[0:15], near_r)
    spot2 = slot_x * 2 + z // 2
    far[spot2] = jnp.sum(near[...], axis=0)
    for dh, dl, dz in [(1, 0, 1), (1, 1, 1), (1, 0, 0), (1, 1, 0), (0, 1, 1), (0, 0, 1), (0, 1, 0)]:
        remote(far.at[spot2], far.at[spot2], far_s, far_r,
               device((xh + dh) % 2, (xl + dl) % 2, y, ztwin if dz else z, core)).start()
    take(far.at[0:7], far_r)

    factors = []
    for x in range(4):
        total = jnp.sum(far[x * 2] + far[x * 2 + 1], axis=(0, 1), keepdims=True)
        factors.append(jnp.minimum(1.0, clip_bound / jnp.sqrt(total + epsilon)) * scaling)

    for k in range(2):
        for x in range(4):
            take(x_got.at[x, k], xs_r.at[x, k])
            take(x_gotstep.at[x, k], xt_r.at[x, k])
        for h in (0, 1):
            total = None
            for x in range(4):
                weight = factors[x] * x_gotstep[x, k, h, 0:1]
                term = x_got[x, k, h].astype(jnp.int32).astype(jnp.float32) * weight
                total = term if total is None else total + term
            out[k * 256:(k + 1) * 256, h * 256:(h + 1) * 256] = total

    for lane in (0, 1):
        src, dst = swap(lane)

        @pl.when(jnp.logical_not(jnp.logical_and(home, core == lane)))
        def _():
            take(src, swap_s.at[lane])

    take(cols.at[0:7, 0:4], ring_s)
    for p in range(4):
        take(cols.at[0], side_s.at[p])
    for slot in range(4):
        @pl.when(home)
        def _():
            take(rows.at[slot, 0:15], rows_s.at[slot])

        @pl.when(jnp.logical_not(home))
        def _():
            take(rows.at[slot], rows_s.at[slot])
    for k in range(2):
        for q in range(8):
            take(t_code.at[q, k], ts_s.at[q, k])
            take(t_step.at[q, k], tt_s.at[q, k])
        for jj in range(4):
            mine = x_parts(k, jj)[0]

            def gone():
                take(x_code.at[k, jj], xs_s.at[k, jj])
                take(x_step.at[k, jj], xt_s.at[k, jj])

            if mine is None:
                gone()
            else:
                pl.when(jnp.logical_not(mine))(gone)
    take(near.at[0:15], near_s)
    take(far.at[0:7], far_s)


def body(hidden, cotangent, lengths):
    tok_count = lax.axis_size("tok")
    user_count = lax.axis_size("user")
    hidden_width = hidden.shape[2]
    model_width = cotangent.shape[2]
    capacity = hidden.shape[1] * tok_count
    clip_bound = math.sqrt(8.0 * hidden_width * model_width * capacity)
    scaling = math.sqrt(hidden_width * model_width) / (user_count * clip_bound)
    half, full, word = jnp.bfloat16, jnp.float32, jnp.int16
    dma = pltpu.SemaphoreType.DMA
    return pl.pallas_call(
        functools.partial(kernel, clip_bound, scaling),
        out_shape=jax.ShapeDtypeStruct((512, 512), full),
        in_specs=[
            pl.BlockSpec(memory_space=pltpu.SMEM),
            pl.BlockSpec(memory_space=pl.ANY),
            pl.BlockSpec(memory_space=pltpu.VMEM),
        ],
        out_specs=pl.BlockSpec(memory_space=pltpu.VMEM),
        scratch_shapes=[
            pltpu.VMEM((8, 128, 256), half),
            pltpu.VMEM((8, 8, 256, 256), half),
            pltpu.VMEM((4, 16, 128, 256), half),
            pltpu.VMEM((4, 256, 2048), half),
            pltpu.VMEM((8, 2, 256, 256), word),
            pltpu.VMEM((8, 2, 8, 256), full),
            pltpu.VMEM((8, 2, 256, 256), word),
            pltpu.VMEM((8, 2, 8, 256), full),
            pltpu.VMEM((2, 4, 2, 256, 256), word),
            pltpu.VMEM((2, 4, 2, 8, 256), full),
            pltpu.VMEM((4, 2, 2, 256, 256), word),
            pltpu.VMEM((4, 2, 2, 8, 256), full),
            pltpu.VMEM((8, 256), full),
            pltpu.VMEM((16, 8, 128), full),
            pltpu.VMEM((8, 8, 128), full),
            dma((2,)), dma((2,)), dma, dma((36,)), dma((4,)), dma((4,)), dma((4,)), dma((4,)),
            dma((8, 2)), dma((8, 2)), dma((8, 2)), dma((8, 2)),
            dma((2, 4)), dma((4, 2)), dma((2, 4)), dma((4, 2)),
            dma, dma, dma, dma,
        ],
        compiler_params=pltpu.CompilerParams(collective_id=0, has_side_effects=True, vmem_limit_bytes=56 << 20),
        name="clipped_sum",
    )(lengths, hidden, cotangent)


def solution(mesh):
    return jax.shard_map(
        body,
        mesh=mesh,
        in_specs=(P("user", "tok", None), P("user", "tok", None), P("user")),
        out_specs=P("tok", "user"),
        check_vma=False,
    )
```

time: 143 us -> 121 us (0.85)
  Pallas kernels: 140 us -> 118 us
    pallas_call x1, Pallas kernels: 140 us -> 118 us  [body(): pl.pallas_call(functools.partial(kernel, clip_bound, scaling), out_shape=...]
where the time goes in v2:
time: 121 us
  Pallas kernels  118 us (98%)
  local copies, waits for them, and re-layouts  2.26 us (2%)
    pallas_call x1, Pallas kernels, body(): pl.pallas_call(functools.partial(kernel, clip_bound, scaling), out_shape=...  118 us

profile of v2, /device:TPU:1, one launch (start us, length us, event | category | flops | bytes accessed | tf_op | source)
XLA Modules:
  0.0 120.8 jit_solution(14759156620978278263)
XLA Ops:
  0.7 117.8 %clipped_sum.1 = f32[512,512]{1,0:T(8,128)} custom-call(s32[1]{0:T(128)S(6)} %copy.5.lengths, bf16[1,128,16384]{2,1,0:T(8,128)(2,1)} %hidden.1, bf16[1,128,2048]{2,1,0:T(8,128)(2,1)} %cotangent.1), custom_call_target="tpu_custom_call" | custom-call | tf_op jit(solution)/shard_map/clipped_sum/pallas_call | solution.py:359
  118.5 2.3 %copy.6 = f32[512,512]{1,0:T(8,128)} copy(f32[512,512]{1,0:T(8,128)} %clipped_sum.1) | data formatting | bytes 2097152

commit v3 on v2

--- a/solution.py
+++ b/solution.py
@@ -11,9 +11,12 @@
 epsilon = 1e-06
 MESH = pl.DeviceIdType.MESH
 LEVELS = 32767.0
+PARTS = 4
+DEEP = 512 // PARTS
 ORDER = [(1, 0, 0), (3, 1, 1), (2, 0, 1), (0, 1, 0), (3, 0, 0), (1, 1, 1), (0, 1, 1), (2, 1, 0),
          (1, 0, 1), (3, 1, 0), (2, 0, 0), (3, 0, 1), (2, 1, 1), (1, 1, 0), (0, 0, 0), (0, 0, 1)]
-PACE = (16, 0, 0, 0, 0, 0, 0, 16, 16, 16, 0, 0, 0)
+PACE = (48, 0, 0, 0, 0, 0, 16, 32, 16, 16, 0, 0)
+SLOTS = [(0, 0), (0, 1), (0, 2), (0, 3), (1, 0), (1, 1), (1, 2), (1, 3)]
 
 
 def device(xh, xl, y, z, core):
@@ -42,9 +45,9 @@
 def kernel(
     clip_bound, scaling,
     lengths, hidden, cotangent, out,
-    masked, cols, rows, turned, t_code, t_step, t_got, t_gotstep,
+    drafts, final, masked, cols, rows, turned, t_code, t_step, t_got, t_gotstep,
     x_code, x_step, x_got, x_gotstep, square, near, far,
-    swap_s, swap_r, ring_s, ring_r, side_s, side_r, rows_s, rows_r,
+    draft_r, swap_s, swap_r, ring_s, ring_r, side_s, side_r, rows_s, rows_r,
     ts_s, ts_r, tt_s, tt_r, xs_s, xs_r, xt_s, xt_r, near_s, near_r, far_s, far_r,
 ):
     user, tok = lax.axis_index("user"), lax.axis_index("tok")
@@ -58,13 +61,13 @@
     shard = zi * 4 + y
 
     def send_row(n):
-        slot, (dy, dz, cc) = n // 16, ORDER[n % 16]
-        kind, k = slot // 2, slot % 2
+        (kind, k), (dy, dz, cc) = SLOTS[n // 16], ORDER[n % 16]
+        slot = kind * PARTS + k
         y2 = (y + dy) % 4
         z2 = zmate if dz else z
         zrow = z2 if kind else 3 - z2
-        start = ((zrow * 4 + y2) * 2 + cc) * 512 + k * 256
-        src = hidden.at[0, :, pl.ds(pl.multiple_of(start, 256), 256)]
+        start = ((zrow * 4 + y2) * 2 + cc) * 512 + k * DEEP
+        src = hidden.at[0, :, pl.ds(pl.multiple_of(start, DEEP), DEEP)]
         dst = rows.at[slot, shard * 2 + xl]
         where = device(xh, core, y2, z2, cc)
         away = remote(src, dst, rows_s.at[slot], rows_r.at[slot], where)
@@ -83,6 +86,8 @@
         for n in range(sum(PACE[:point]), sum(PACE[:point + 1])):
             send_row(n)
 
+    draft = pltpu.make_async_copy(cotangent.at[0], drafts, draft_r)
+    draft.start()
     barrier = pltpu.get_barrier_semaphore()
     partners = [(xh, (xl + dl) % 2, (y + dy) % 4, z2, (core + dc) % 2)
                 for dl in range(2) for dy in range(4) for z2 in (z, zmate) for dc in range(2)][1:]
@@ -93,10 +98,11 @@
 
     token = tok * 128 + lax.broadcasted_iota(jnp.int32, (128, 256), 0)
     keep = token < lengths[0]
+    draft.wait()
     for q in range(8):
         lane, p = q // 4, q % 4
         start = (((1 - xh if p < 2 else xh) * 2 + lane) * 2 + p % 2) * 256
-        part = cotangent[0, :, pl.ds(pl.multiple_of(start, 256), 256)]
+        part = drafts[:, pl.ds(pl.multiple_of(start, 256), 256)]
         masked[q] = jnp.where(keep, part, jnp.zeros((128, 256), jnp.bfloat16))
 
     pl.semaphore_wait(barrier, len(partners))
@@ -201,17 +207,17 @@
     def t_scale(q, k):
         return remote(t_step.at[q, k], t_gotstep.at[q, k], tt_s.at[q, k], tt_r.at[q, k], twin)
 
-    def t_part(p, k):
-        def one(lane, carry):
-            q = lane * 4 + p
-            code, step = coded(product(turned[k], q))
-            t_code[q, k] = code
-            t_step[q, k] = jnp.broadcast_to(step, (8, 256))
-            t_data(q, k).start()
-            t_scale(q, k).start()
-            return carry
-
-        lax.fori_loop(0, 2, one, 0)
+    def both(slot):
+        return turned[slot:slot + 2].reshape(2 * DEEP, 2048)
+
+    def t_two(q, k):
+        value = product(both(k), q)
+        for i in (0, 1):
+            code, step = coded(value[i * DEEP:(i + 1) * DEEP])
+            t_code[q, k + i] = code
+            t_step[q, k + i] = step
+            t_data(q, k + i).start()
+            t_scale(q, k + i).start()
 
     for tick in range(8):
         for lane, steps in enumerate((lane0, lane1)):
@@ -223,14 +229,16 @@
         send_rows(1 + tick)
         if tick == 4:
             turn(0)
+            turn(1)
         if tick >= 4:
             take(cols.at[0], side_r.at[tick - 4])
-            t_part(tick - 4, 0)
-
-    turn(1)
-    for p in range(4):
-        send_rows(9 + p)
-        t_part(p, 1)
+
+
+            def one(lane, carry, tick=tick):
+                t_two(lane * 4 + tick - 4, 0)
+                return carry
+
+            lax.fori_loop(0, 2, one, 0)
 
     square[...] = jnp.zeros_like(square)
     slot_x = xh * 2 + xl
@@ -243,40 +251,84 @@
         scale = (x_step.at[k, jj], x_gotstep.at[slot_x, k])
         return mine, where, data, scale
 
-    def o_pass(k, carry):
-        turn(2 + k)
-        for jj in range(4):
-            def one(h, inner, jj=jj):
-                q = (jj % 2) * 4 + (jj // 2) * 2 + h
-                value = product(turned[2 + k], q)
-                take(t_got.at[q, k], ts_r.at[q, k])
-                take(t_gotstep.at[q, k], tt_r.at[q, k])
-                value = value + t_got[q, k].astype(jnp.int32).astype(jnp.float32) * t_gotstep[q, k, 0:1]
-                square[...] += jnp.sum((value * value).reshape(32, 8, 256), axis=0)
-                code, step = coded(value)
-                x_code[k, jj, h] = code
-                x_step[k, jj, h] = jnp.broadcast_to(step, (8, 256))
-                return inner
-
-            lax.fori_loop(0, 2, one, 0)
-            mine, where, data, scale = x_parts(k, jj)
-
-            def away():
-                remote(*data, xs_s.at[k, jj], xs_r.at[slot_x, k], where).start()
-                remote(*scale, xt_s.at[k, jj], xt_r.at[slot_x, k], where).start()
-
-            def near_by():
-                pltpu.make_async_copy(*data, xs_r.at[slot_x, k]).start()
-                pltpu.make_async_copy(*scale, xt_r.at[slot_x, k]).start()
-
-            if mine is None:
-                away()
-            else:
-                pl.when(mine)(near_by)
-                pl.when(jnp.logical_not(mine))(away)
+    def o_sum(k, q, value):
+        take(t_got.at[q, k], ts_r.at[q, k])
+        take(t_gotstep.at[q, k], tt_r.at[q, k])
+        value = value + t_got[q, k].astype(jnp.int32).astype(jnp.float32) * t_gotstep[q, k]
+        square[...] += jnp.sum((value * value).reshape(DEEP // 8, 8, 256), axis=0)
+        return value
+
+    def o_at(jj, h):
+        return (jj % 2) * 4 + (jj // 2) * 2 + h
+
+    def o_code(k, jj, h, value):
+        code, step = coded(value)
+        x_code[k, jj, h] = code
+        x_step[k, jj, h] = step
+
+    def o_send(k, jj):
+        mine, where, data, scale = x_parts(k, jj)
+
+        def away():
+            remote(*data, xs_s.at[k, jj], xs_r.at[slot_x, k], where).start()
+            remote(*scale, xt_s.at[k, jj], xt_r.at[slot_x, k], where).start()
+
+        def near_by():
+            pltpu.make_async_copy(*data, xs_r.at[slot_x, k]).start()
+            pltpu.make_async_copy(*scale, xt_r.at[slot_x, k]).start()
+
+        if mine is None:
+            away()
+        else:
+            pl.when(mine)(near_by)
+            pl.when(jnp.logical_not(mine))(away)
+
+    send_rows(9)
+    turn(2)
+    turn(3)
+
+    def late(n, carry):
+        t_two((n % 2) * 4 + n // 2, 2)
         return carry
 
-    lax.fori_loop(0, 2, o_pass, 0)
+    lax.fori_loop(0, 8, late, 0)
+    send_rows(10)
+
+    turn(PARTS)
+    turn(PARTS + 1)
+    for jj in range(4):
+        def one(h, carry, jj=jj):
+            q = o_at(jj, h)
+            value = product(both(PARTS), q)
+            for i in (0, 1):
+                o_code(i, jj, h, o_sum(i, q, value[i * DEEP:(i + 1) * DEEP]))
+            return carry
+
+        lax.fori_loop(0, 2, one, 0)
+        o_send(0, jj)
+        o_send(1, jj)
+    send_rows(11)
+
+    turn(PARTS + 2)
+    for jj in range(4):
+        def one(h, carry, jj=jj):
+            q = o_at(jj, h)
+            o_code(2, jj, h, o_sum(2, q, product(turned[PARTS + 2], q)))
+            return carry
+
+        lax.fori_loop(0, 2, one, 0)
+        o_send(2, jj)
+
+    last = PARTS - 1
+    turn(PARTS + last)
+
+    def draft_of(n, carry):
+        jj, h = n // 2, n % 2
+        q = o_at(jj, h)
+        final[n] = o_sum(last, q, product(turned[PARTS + last], q))
+        return carry
+
+    lax.fori_loop(0, 8, draft_of, 0)
 
     spot1 = shard * 2 + core
     near[spot1] = square[:, 0:128] + square[:, 128:256]
@@ -284,6 +336,14 @@
                        (1, 0, 1), (3, 0, 1), (1, 0, 0), (3, 0, 0), (0, 1, 1), (0, 1, 0), (0, 0, 1)]:
         remote(near.at[spot1], near.at[spot1], near_s, near_r,
                device(xh, xl, (y + dy) % 4, zmate if dz else z, (core + dc) % 2)).start()
+    for jj in range(4):
+        def one(h, carry, jj=jj):
+            o_code(last, jj, h, final[jj * 2 + h])
+            return carry
+
+        lax.fori_loop(0, 2, one, 0)
+        o_send(last, jj)
+
     take(near.at[0:15], near_r)
     spot2 = slot_x * 2 + z // 2
     far[spot2] = jnp.sum(near[...], axis=0)
@@ -297,17 +357,17 @@
         total = jnp.sum(far[x * 2] + far[x * 2 + 1], axis=(0, 1), keepdims=True)
         factors.append(jnp.minimum(1.0, clip_bound / jnp.sqrt(total + epsilon)) * scaling)
 
-    for k in range(2):
+    for k in range(PARTS):
         for x in range(4):
             take(x_got.at[x, k], xs_r.at[x, k])
             take(x_gotstep.at[x, k], xt_r.at[x, k])
         for h in (0, 1):
             total = None
             for x in range(4):
-                weight = factors[x] * x_gotstep[x, k, h, 0:1]
+                weight = factors[x] * x_gotstep[x, k, h]
                 term = x_got[x, k, h].astype(jnp.int32).astype(jnp.float32) * weight
                 total = term if total is None else total + term
-            out[k * 256:(k + 1) * 256, h * 256:(h + 1) * 256] = total
+            out[k * DEEP:(k + 1) * DEEP, h * 256:(h + 1) * 256] = total
 
     for lane in (0, 1):
         src, dst = swap(lane)
@@ -319,7 +379,7 @@
     take(cols.at[0:7, 0:4], ring_s)
     for p in range(4):
         take(cols.at[0], side_s.at[p])
-    for slot in range(4):
+    for slot in range(2 * PARTS):
         @pl.when(home)
         def _():
             take(rows.at[slot, 0:15], rows_s.at[slot])
@@ -327,7 +387,7 @@
         @pl.when(jnp.logical_not(home))
         def _():
             take(rows.at[slot], rows_s.at[slot])
-    for k in range(2):
+    for k in range(PARTS):
         for q in range(8):
             take(t_code.at[q, k], ts_s.at[q, k])
             take(t_step.at[q, k], tt_s.at[q, k])
@@ -362,28 +422,30 @@
         in_specs=[
             pl.BlockSpec(memory_space=pltpu.SMEM),
             pl.BlockSpec(memory_space=pl.ANY),
-            pl.BlockSpec(memory_space=pltpu.VMEM),
+            pl.BlockSpec(memory_space=pl.ANY),
         ],
         out_specs=pl.BlockSpec(memory_space=pltpu.VMEM),
         scratch_shapes=[
+            pltpu.VMEM((128, 2048), half),
+            pltpu.VMEM((8, DEEP, 256), full),
             pltpu.VMEM((8, 128, 256), half),
             pltpu.VMEM((8, 8, 256, 256), half),
-            pltpu.VMEM((4, 16, 128, 256), half),
-            pltpu.VMEM((4, 256, 2048), half),
-            pltpu.VMEM((8, 2, 256, 256), word),
-            pltpu.VMEM((8, 2, 8, 256), full),
-            pltpu.VMEM((8, 2, 256, 256), word),
-            pltpu.VMEM((8, 2, 8, 256), full),
-            pltpu.VMEM((2, 4, 2, 256, 256), word),
-            pltpu.VMEM((2, 4, 2, 8, 256), full),
-            pltpu.VMEM((4, 2, 2, 256, 256), word),
-            pltpu.VMEM((4, 2, 2, 8, 256), full),
+            pltpu.VMEM((2 * PARTS, 16, 128, DEEP), half),
+            pltpu.VMEM((2 * PARTS, DEEP, 2048), half),
+            pltpu.VMEM((8, PARTS, DEEP, 256), word),
+            pltpu.VMEM((8, PARTS, 1, 256), full),
+            pltpu.VMEM((8, PARTS, DEEP, 256), word),
+            pltpu.VMEM((8, PARTS, 1, 256), full),
+            pltpu.VMEM((PARTS, 4, 2, DEEP, 256), word),
+            pltpu.VMEM((PARTS, 4, 2, 1, 256), full),
+            pltpu.VMEM((4, PARTS, 2, DEEP, 256), word),
+            pltpu.VMEM((4, PARTS, 2, 1, 256), full),
             pltpu.VMEM((8, 256), full),
             pltpu.VMEM((16, 8, 128), full),
             pltpu.VMEM((8, 8, 128), full),
-            dma((2,)), dma((2,)), dma, dma((36,)), dma((4,)), dma((4,)), dma((4,)), dma((4,)),
-            dma((8, 2)), dma((8, 2)), dma((8, 2)), dma((8, 2)),
-            dma((2, 4)), dma((4, 2)), dma((2, 4)), dma((4, 2)),
+            dma, dma((2,)), dma((2,)), dma, dma((36,)), dma((4,)), dma((4,)), dma((2 * PARTS,)), dma((2 * PARTS,)),
+            dma((8, PARTS)), dma((8, PARTS)), dma((8, PARTS)), dma((8, PARTS)),
+            dma((PARTS, 4)), dma((4, PARTS)), dma((PARTS, 4)), dma((4, PARTS)),
             dma, dma, dma, dma,
         ],
         compiler_params=pltpu.CompilerParams(collective_id=0, has_side_effects=True, vmem_limit_bytes=56 << 20),

time: 121 us -> 117 us (0.967)
  Pallas kernels: 118 us -> 114 us
    pallas_call x1, Pallas kernels: 118 us -> 114 us  [body(): pl.pallas_call(functools.partial(kernel, clip_bound, scaling), out_shape=...]
where the time goes in v3:
time: 117 us
  Pallas kernels  114 us (97%)
  local copies, waits for them, and re-layouts  2.26 us (2%)
    pallas_call x1, Pallas kernels, body(): pl.pallas_call(functools.partial(kernel, clip_bound, scaling), out_shape=...  114 us

profile of v3, /device:TPU:1, one launch (start us, length us, event | category | flops | bytes accessed | tf_op | source)
XLA Modules:
  0.0 117.0 jit_solution(17273800326719186591)
XLA Ops:
  0.7 114.1 %clipped_sum.1 = f32[512,512]{1,0:T(8,128)} custom-call(s32[1]{0:T(128)S(6)} %copy.5.lengths, bf16[1,128,16384]{2,1,0:T(8,128)(2,1)} %hidden.1, bf16[1,128,2048]{2,1,0:T(8,128)(2,1)} %cotangent.1), custom_call_target="tpu_custom_call" | custom-call | tf_op jit(solution)/shard_map/clipped_sum/pallas_call | solution.py:419
  114.7 2.3 %copy.6 = f32[512,512]{1,0:T(8,128)} copy(f32[512,512]{1,0:T(8,128)} %clipped_sum.1) | data formatting | bytes 2097152

commit v4 on v3

--- a/solution.py
+++ b/solution.py
@@ -63,7 +63,7 @@
     def send_row(n):
         (kind, k), (dy, dz, cc) = SLOTS[n // 16], ORDER[n % 16]
         slot = kind * PARTS + k
-        y2 = (y + dy) % 4
+        y2 = (y + dy * (1 + 2 * core)) % 4
         z2 = zmate if dz else z
         zrow = z2 if kind else 3 - z2
         start = ((zrow * 4 + y2) * 2 + cc) * 512 + k * DEEP

time: 117 us -> 117 us (level)
  no operation moved by 1% of the time
where the time goes in v4:
time: 117 us
  Pallas kernels  114 us (97%)
  local copies, waits for them, and re-layouts  2.26 us (2%)
    pallas_call x1, Pallas kernels, body(): pl.pallas_call(functools.partial(kernel, clip_bound, scaling), out_shape=...  114 us

profile of v4, /device:TPU:1, one launch (start us, length us, event | category | flops | bytes accessed | tf_op | source)
XLA Modules:
  0.0 117.0 jit_solution(373756900847773652)
XLA Ops:
  0.7 114.0 %clipped_sum.1 = f32[512,512]{1,0:T(8,128)} custom-call(s32[1]{0:T(128)S(6)} %copy.5.lengths, bf16[1,128,16384]{2,1,0:T(8,128)(2,1)} %hidden.1, bf16[1,128,2048]{2,1,0:T(8,128)(2,1)} %cotangent.1), custom_call_target="tpu_custom_call" | custom-call | tf_op jit(solution)/shard_map/clipped_sum/pallas_call | solution.py:419
  114.7 2.3 %copy.6 = f32[512,512]{1,0:T(8,128)} copy(f32[512,512]{1,0:T(8,128)} %clipped_sum.1) | data formatting | bytes 2097152
